TPU v7x, 32 devices: a whole 2x2x4 slice. The times are simulated.
32 devices in a mesh: bpm: 4 (over y, x), cor: 8 (over z, core).
Axes of the slice: x: 2, y: 2, z: 4, core: 2. Of those that a mesh axis runs over, the one named last changes fastest.
Arguments:
- quad_bpm: bfloat16 [6144, 2048], P('cor', 'bpm'), may hold values from -0.078125 to 0.078125
- cor_quad: bfloat16 [6144, 6144], P('cor', 'bpm'), may hold values from -0.875 to 0.875
- step: float32 [6144], P(('bpm', 'cor')), may hold values from -6 to 6
- quad_order: int32 [6144], replicated, may hold values from 0 to 6143, each once
- bpm_mask: int32 [2048], P('bpm'), may hold values 0 or 1
- bpm_noise: float32 [2048], P('bpm'), may hold values from 0.5 to 2
Outputs:
- product: float32 [6144], P(('bpm', 'cor'))
Inputs may be any that keep to these rules, and one draw needn't show every extreme that they name: `quad_order`: each parameter drives exactly one quadrupole.
All inputs are finite; a program needn't handle non-finite values. No bound on the sum of `bpm_mask` on one device may be relied on, other than what follows from the above.
Results may differ from a plain program's by a relative error of at most 0.00035.
Values may be sent and summed in bfloat16 or wider, within the bound.
No kernel may reach another device: no remote copies, remote signals or barrier semaphores. Data moves between devices by JAX's collectives and lax.ppermute only.
A program may use at most 64 MiB of HBM per device.

v0:
```python
import jax
import jax.numpy as jnp
from jax import lax
from jax.sharding import PartitionSpec as P


def on_device(quad_bpm, cor_quad, step, quad_order, bpm_mask, bpm_noise):
    whole_step = lax.all_gather(step, ("bpm", "cor"), axis=0, tiled=True)
    u_vec = whole_step[quad_order]
    sens_full = lax.all_gather(cor_quad, "bpm", axis=1, tiled=True)
    scaled = (u_vec[None, :] * sens_full.astype(jnp.float32)).astype(jnp.bfloat16)
    weight = bpm_mask.astype(jnp.float32) / (bpm_noise * bpm_noise)
    rows_full = lax.all_gather(quad_bpm, "cor", axis=0, tiled=True)
    response = jnp.dot(scaled, rows_full, preferred_element_type=jnp.float32)
    weighted = (weight[None, :] * response).astype(jnp.bfloat16)
    back = lax.dot_general(
        sens_full, weighted, (((0,), (0,)), ((), ())), preferred_element_type=jnp.float32
    )
    d_vec = jnp.sum(rows_full.astype(jnp.float32) * back, axis=1)
    partial_value = jnp.zeros((quad_order.shape[0],), jnp.float32).at[quad_order].set(d_vec)
    total = lax.psum(partial_value, ("bpm", "cor"))
    share = step.shape[0]
    return lax.dynamic_slice_in_dim(total, lax.axis_index(("bpm", "cor")) * share, share, 0)


def solution(mesh):
    placed = (P("cor", "bpm"), P("cor", "bpm"), P(("bpm", "cor")), P(), P("bpm"), P("bpm"))
    return jax.shard_map(
        on_device, mesh=mesh, in_specs=placed, out_specs=P(("bpm", "cor")), check_vma=False
    )
```

profile of v0, /device:TPU:0, one launch (start us, length us, event | category | flops | bytes accessed | tf_op | source)
XLA Modules:
  0.0 260.7 jit_solution(18259405172421799365)
XLA Ops:
  6.5 0.0 all-gather.3.cloned.1.call-start
  6.5 2.3 copy.8
  8.8 0.0 all-gather.3.cloned.1.call-update
  8.9 0.0 all-gather.5.cloned.1.call-start
  8.9 0.7 all-gather.5.cloned.1.call-update
  9.6 0.9 dynamic-update-slice
  10.5 46.3 %all-reduce = f32[6144]{0:T(1024)S(1)} all-reduce(f32[6144]{0:T(1024)S(1)} %dynamic-update-slice), channel_id=1, replica_groups=mesh['bpm'=4,'cor'=8] {'bpm','cor'}, use_global_device_ids=true, to_apply=%add | all-reduce | flops 6144 | bytes 49152
  56.8 0.7 broadcast_clamp_fusion
  57.6 0.0 copy-start
  57.6 0.0 copy-start.1
  57.6 34.3 %gather_fusion = f32[6144]{0:T(1024)S(1)} fusion(f32[6144]{0:T(1024)S(1)} %all-reduce, s32[6144]{0:T(1024)S(1)} %get-tuple-element.5), kind=kCustom, calls=%fused_computation | custom fusion | bytes 73728 | tf_op jit(solution)/shard_map/gather | solution.py:9
  91.9 0.0 copy-done
  91.9 0.0 copy-done.1
  91.9 0.0 all-gather.3.cloned.1.call-done
  92.0 82.1 %all-gather.5.cloned.1.call-done = bf16[768,6144]{1,0:T(8,128)(2,1)} async-done(((bf16[768,1536]{1,0:T(8,128)(2,1)}), bf16[768,6144]{1,0:T(8,128)(2,1)}) %all-gather.5.cloned.1.call-update) | async-done | bytes 9437200 | tf_op jit(solution)/shard_map/all_gather | solution.py:10
  174.1 0.0 copy-start.2
  174.1 0.0 copy-start.3
  174.1 10.6 %multiply_convert_fusion.2 = bf16[768,512]{1,0:T(8,128)(2,1)S(1)} fusion(bf16[6144,512]{0,1:T(8,128)(2,1)} %all-gather.3.cloned.1.call-done, bf16[768,6144]{1,0:T(8,128)(2,1)} %all-gather.5.cloned.1.call-done, f32[6144]{0:T(1024)S(1)} %gather_fusion, f32[512]{0:T(512)S(1)} %multiply_divide_fusion), kind=kOutput, calls=%fused_computation.7 | convolution fusion | flops 4846780416 | bytes 16541696 | tf_op jit(solution)/shard_map/dot_general | solution.py:14
  184.7 0.0 copy-done.2
  184.7 0.0 copy-done.3
  184.8 5.9 %fusion = f32[6144]{0:T(1024)S(1)} fusion(bf16[6144,512]{0,1:T(8,128)(2,1)S(1)} %copy-done.3, bf16[768,512]{1,0:T(8,128)(2,1)S(1)} %multiply_convert_fusion.2, bf16[768,6144]{1,0:T(8,128)(2,1)S(1)} %copy-done.2), kind=kOutput, calls=%fused_computation.4 | convolution fusion | flops 4841269248 | bytes 16539648 | tf_op jit(solution)/shard_map/dot_general | solution.py:16
  190.7 23.0 %scatter_custom_fusion = f32[6144]{0:T(1024)S(1)} fusion(s32[6144]{0:T(1024)S(1)} %get-tuple-element.6, f32[6144]{0:T(1024)S(1)} %fusion, f32[]{:T(128)} %constant.7.clone.1), kind=kCustom, calls=%fused_computation.10 | custom fusion | bytes 24580 | tf_op jit(solution)/shard_map/scatter | solution.py:20
  213.7 39.5 %psum.7 = f32[6144]{0:T(1024)S(1)} all-reduce(f32[6144]{0:T(1024)S(1)} %scatter_custom_fusion), channel_id=1, replica_groups=mesh['bpm'=4,'cor'=8] {'bpm','cor'}, use_global_device_ids=true, to_apply=%region_2.0 | all-reduce | flops 6144 | bytes 49152 | tf_op jit(solution)/shard_map/psum | solution.py:21
  253.2 0.6 dynamic_slice.3
  (2 shorter events, 0.0 us)
Async XLA Ops:
  6.5 85.4 %all-gather.3.cloned.1.call-start = ((), (), s32[]{:S(2)}) async-start(), calls=%async_computation | async-start | bytes 7077888 | tf_op jit(solution)/shard_map/all_gather | solution.py:13
  8.9 165.2 %all-gather.5.cloned.1.call-start = ((), (), s32[]{:S(2)}) async-start(), calls=%async_computation.1 | async-start | bytes 11796480 | tf_op jit(solution)/shard_map/all_gather | solution.py:10
  57.6 34.3 %copy-start = (f32[512]{0:T(512)S(1)}, f32[512]{0:T(512)}, u32[]{:S(2)}) copy-start(f32[512]{0:T(512)} %param.11) | copy-start | bytes 6148
  57.6 34.3 %copy-start.1 = (s32[512]{0:T(512)S(1)}, s32[512]{0:T(512)}, u32[]{:S(2)}) copy-start(s32[512]{0:T(512)} %param.10) | copy-start | bytes 6148
  174.1 10.6 %copy-start.2 = (bf16[768,6144]{1,0:T(8,128)(2,1)S(1)}, bf16[768,6144]{1,0:T(8,128)(2,1)}, u32[]{:S(2)}) copy-start(bf16[768,6144]{1,0:T(8,128)(2,1)} %all-gather.5.cloned.1.call-done) | copy-start | bytes 28311556
  174.1 10.6 %copy-start.3 = (bf16[6144,512]{0,1:T(8,128)(2,1)S(1)}, bf16[6144,512]{0,1:T(8,128)(2,1)}, u32[]{:S(2)}) copy-start(bf16[6144,512]{0,1:T(8,128)(2,1)} %all-gather.3.cloned.1.call-done) | copy-start | bytes 18874372
Sparse Core Ops, SparseCore 0:
  9.0 68.3 all-gather.2
  79.2 94.8 all-gather.4
where the time goes:
time: 261 us
  blocking collectives  85.8 us (33%)
  waiting for transfers between devices  82.9 us (32%)
  local copies, waits for them, and re-layouts  61.2 us (23%)
  matrix products  16.5 us (6%)
  between operations  13.5 us (5%)
    all_gather x1, waiting for transfers between devices, on_device(): sens_full = lax.all_gather(cor_quad, 'bpm', axis=1, tiled=True)  82.1 us
    unnamed x1, blocking collectives  46.3 us
    psum x1, blocking collectives, on_device(): total = lax.psum(partial_value, ('bpm', 'cor'))  39.5 us
    gather x1, local copies, waits for them, and re-layouts, on_device(): u_vec = whole_step[quad_order]  34.3 us
    scatter x1, local copies, waits for them, and re-layouts, on_device(): jnp.zeros((quad_order.shape[0],), jnp.float32).at[quad_order].set(d_vec)  23 us
    dot_general x1, matrix products, on_device(): response = jnp.dot(scaled, rows_full, preferred_element_type=jnp.float32)  10.6 us
    dot_general x1, matrix products, on_device(): lax.dot_general(sens_full, weighted, (((0,), (0,)), ((), ())), preferred_...  5.92 us
  transfers between devices with their start and end apart: 2, of which 1 were waited for; matrix products, arithmetic and copies ran while one was open for 14% of the time, Pallas kernels for 0%

commit v1 on v0

--- a/solution.py
+++ b/solution.py
@@ -7,7 +7,9 @@
 def on_device(quad_bpm, cor_quad, step, quad_order, bpm_mask, bpm_noise):
     whole_step = lax.all_gather(step, ("bpm", "cor"), axis=0, tiled=True)
     u_vec = whole_step[quad_order]
-    sens_full = lax.all_gather(cor_quad, "bpm", axis=1, tiled=True)
+    sens_full = jnp.concatenate(
+        lax.all_to_all(jnp.stack([cor_quad] * lax.axis_size("bpm")), "bpm", 0, 0), axis=1
+    )
     scaled = (u_vec[None, :] * sens_full.astype(jnp.float32)).astype(jnp.bfloat16)
     weight = bpm_mask.astype(jnp.float32) / (bpm_noise * bpm_noise)
     rows_full = lax.all_gather(quad_bpm, "cor", axis=0, tiled=True)

time: 261 us -> 297 us (1.14)
  blocking collectives: 85.8 us -> 179 us
  waiting for transfers between devices: 82.9 us -> 0.02 us
  local copies, waits for them, and re-layouts: 61.2 us -> 79.3 us
  starting transfers between devices: 0.04 us -> 6.07 us
    unnamed x1, blocking collectives: 46.3 us -> 139 us
    all_gather x1 -> x0, waiting for transfers between devices: 82.1 us -> none  [on_device(): sens_full = lax.all_gather(cor_quad, 'bpm', axis=1, tiled=True)]
    all_to_all x0 -> x1, local copies, waits for them, and re-layouts: none -> 12.7 us  [on_device(): lax.all_to_all(jnp.stack([cor_quad] * lax.axis_size('bpm')), 'bpm', 0, 0)]
    all_to_all x0 -> x1, starting transfers between devices: none -> 6.07 us  [on_device(): lax.all_to_all(jnp.stack([cor_quad] * lax.axis_size('bpm')), 'bpm', 0, 0)]
    another operation x0 -> x1, local copies, waits for them, and re-layouts: none -> 6.05 us  [on_device(): jnp.stack([cor_quad] * lax.axis_size('bpm'))]
  transfers between devices with their start and end apart: 2 -> 2, of which waited for: 1 -> 0; matrix products, arithmetic and copies ran while one was open for 14% -> 18% of each run, Pallas kernels for 0% -> 0%
where the time goes in v1:
time: 297 us; the launch traced here: 296 us
  blocking collectives  179 us (60%)
  local copies, waits for them, and re-layouts  79.3 us (27%)
  matrix products  18.8 us (6%)
  between operations  13.5 us (5%)
  starting transfers between devices  6.07 us (2%)
    unnamed x1, blocking collectives  139 us
    psum x1, blocking collectives, on_device(): total = lax.psum(partial_value, ('bpm', 'cor'))  39.2 us
    gather x1, local copies, waits for them, and re-layouts, on_device(): u_vec = whole_step[quad_order]  34.3 us
    scatter x1, local copies, waits for them, and re-layouts, on_device(): jnp.zeros((quad_order.shape[0],), jnp.float32).at[quad_order].set(d_vec)  23 us
    all_to_all x1, local copies, waits for them, and re-layouts, on_device(): lax.all_to_all(jnp.stack([cor_quad] * lax.axis_size('bpm')), 'bpm', 0, 0)  12.7 us
    dot_general x1, matrix products, on_device(): response = jnp.dot(scaled, rows_full, preferred_element_type=jnp.float32)  11.6 us
    dot_general x1, matrix products, on_device(): lax.dot_general(sens_full, weighted, (((0,), (0,)), ((), ())), preferred_...  7.23 us
    all_to_all x1, starting transfers between devices, on_device(): lax.all_to_all(jnp.stack([cor_quad] * lax.axis_size('bpm')), 'bpm', 0, 0)  6.07 us
  transfers between devices with their start and end apart: 2, of which 0 were waited for; matrix products, arithmetic and copies ran while one was open for 18% of the time, Pallas kernels for 0%

profile of v1, /device:TPU:0, one launch (start us, length us, event | category | flops | bytes accessed | tf_op | source)
XLA Modules:
  0.0 296.4 jit_solution(5007670301437909283)
XLA Ops:
  6.5 0.0 all-gather.2.cloned.1.call-start
  6.5 2.3 copy.10
  8.9 0.0 all-gather.2.cloned.1.call-update
  8.9 6.0 %stack.2 = bf16[4,768,1536]{2,1,0:T(8,128)(2,1)} broadcast(bf16[768,1536]{1,0:T(8,128)(2,1)} %param.7), dimensions={1,2} | broadcast | bytes 11796480 | tf_op jit(solution)/shard_map/stack | solution.py:11
  14.9 0.0 copy-start.4
  15.0 0.0 copy-start.1
  15.0 6.1 %all-to-all-start = ((bf16[4,768,1536]{2,1,0:T(8,128)(2,1)}), bf16[4,768,1536]{2,1,0:T(8,128)(2,1)}, u32[]{:S(2)}, u32[]{:S(2)}) async-start(bf16[4,768,1536]{2,1,0:T(8,128)(2,1)} %stack.2), calls=%async_computation | async-start | bytes 18874368 | tf_op jit(solution)/shard_map/all_to_all | solution.py:11
  21.1 0.0 copy-done.4
  21.1 0.3 dynamic-update-slice
  21.3 139.4 %all-reduce = f32[6144]{0:T(1024)S(1)} all-reduce(f32[6144]{0:T(1024)S(1)} %dynamic-update-slice), channel_id=1, replica_groups=mesh['bpm'=4,'cor'=8] {'bpm','cor'}, use_global_device_ids=true, to_apply=%add | all-reduce | flops 6144 | bytes 49152
  160.7 0.0 copy-done.1
  160.7 0.0 copy-start.2
  160.8 0.0 copy-start.3
  160.8 34.3 %gather_fusion = f32[6144]{0:T(1024)S(1)} fusion(f32[6144]{0:T(1024)S(1)} %all-reduce, s32[6144]{0:T(1024)S(1)} %get-tuple-element.5), kind=kCustom, calls=%fused_computation | custom fusion | bytes 73728 | tf_op jit(solution)/shard_map/gather | solution.py:9
  195.1 0.0 copy-done.2
  195.1 0.0 copy-done.3
  195.1 0.0 all-to-all-done
  195.1 12.7 %copy.11 = bf16[4,768,1536]{1,2,0:T(8,128)(2,1)} copy(bf16[4,768,1536]{2,1,0:T(8,128)(2,1)} %all-to-all-done) | data formatting | bytes 18874368 | tf_op jit(solution)/shard_map/all_to_all | solution.py:11
  207.8 0.0 all-gather.2.cloned.1.call-done
  207.8 0.0 copy-start
  207.8 11.6 %multiply_convert_fusion.2 = bf16[768,512]{1,0:T(8,128)(2,1)S(1)} fusion(bf16[6144,512]{0,1:T(8,128)(2,1)} %all-gather.2.cloned.1.call-done, bf16[768,6144]{0,1:T(8,128)(2,1)} %bitcast.10, f32[6144]{0:T(1024)S(1)} %gather_fusion, f32[512]{0:T(512)S(1)} %multiply_divide_fusion), kind=kOutput, calls=%fused_computation.7 | convolution fusion | flops 4846780416 | bytes 16541696 | tf_op jit(solution)/shard_map/dot_general | solution.py:16
  219.4 0.0 copy-done
  219.4 7.2 %fusion = f32[6144]{0:T(1024)S(1)} fusion(bf16[6144,512]{0,1:T(8,128)(2,1)} %all-gather.2.cloned.1.call-done, bf16[768,512]{1,0:T(8,128)(2,1)S(1)} %multiply_convert_fusion.2, bf16[768,6144]{0,1:T(8,128)(2,1)S(1)} %bitcast.11), kind=kOutput, calls=%fused_computation.4 | convolution fusion | flops 4841269248 | bytes 16539648 | tf_op jit(solution)/shard_map/dot_general | solution.py:18
  226.7 23.0 %scatter_custom_fusion = f32[6144]{0:T(1024)S(1)} fusion(s32[6144]{0:T(1024)S(1)} %get-tuple-element.6, f32[6144]{0:T(1024)S(1)} %fusion, f32[]{:T(128)} %constant.7.clone.1), kind=kCustom, calls=%fused_computation.10 | custom fusion | bytes 24580 | tf_op jit(solution)/shard_map/scatter | solution.py:22
  249.7 39.2 %psum.7 = f32[6144]{0:T(1024)S(1)} all-reduce(f32[6144]{0:T(1024)S(1)} %scatter_custom_fusion), channel_id=1, replica_groups=mesh['bpm'=4,'cor'=8] {'bpm','cor'}, use_global_device_ids=true, to_apply=%region_2.0 | all-reduce | flops 6144 | bytes 49152 | tf_op jit(solution)/shard_map/psum | solution.py:23
  288.9 0.6 dynamic_slice.3
  (3 shorter events, 0.0 us)
Async XLA Ops:
  6.5 201.3 %all-gather.2.cloned.1.call-start = ((), (), s32[]{:S(2)}) async-start(), calls=%async_computation.1 | async-start | bytes 7077888 | tf_op jit(solution)/shard_map/all_gather | solution.py:15
  14.9 6.1 %copy-start.4 = (f32[192]{0:T(256)S(1)}, f32[192]{0:T(256)}, u32[]{:S(2)}) copy-start(f32[192]{0:T(256)} %param.8) | copy-start | bytes 2308
  15.0 145.8 %copy-start.1 = (s32[6144]{0:T(1024)S(1)}, s32[6144]{0:T(1024)}, u32[]{:S(2)}) copy-start(s32[6144]{0:T(1024)} %param.9) | copy-start | bytes 73732
  15.0 180.1 %all-to-all-start = ((bf16[4,768,1536]{2,1,0:T(8,128)(2,1)}), bf16[4,768,1536]{2,1,0:T(8,128)(2,1)}, u32[]{:S(2)}, u32[]{:S(2)}) async-start(bf16[4,768,1536]{2,1,0:T(8,128)(2,1)} %stack.2), calls=%async_computation | async-start | bytes 18874368 | tf_op jit(solution)/shard_map/all_to_all | solution.py:11
  160.7 34.3 %copy-start.2 = (f32[512]{0:T(512)S(1)}, f32[512]{0:T(512)}, u32[]{:S(2)}) copy-start(f32[512]{0:T(512)} %param.11) | copy-start | bytes 6148
  160.8 34.3 %copy-start.3 = (s32[512]{0:T(512)S(1)}, s32[512]{0:T(512)}, u32[]{:S(2)}) copy-start(s32[512]{0:T(512)} %param.10) | copy-start | bytes 6148
  207.8 11.6 %copy-start = (bf16[4,768,1536]{1,2,0:T(8,128)(2,1)S(1)}, bf16[4,768,1536]{1,2,0:T(8,128)(2,1)}, u32[]{:S(2)}) copy-start(bf16[4,768,1536]{1,2,0:T(8,128)(2,1)} %copy.11) | copy-start | bytes 28311556
Sparse Core Ops, SparseCore 0:
  9.0 67.4 all-gather.1
